TPU v7x, 32 devices: a whole 2x2x4 slice. The times are simulated.
32 devices in a mesh: seq: 8 (over y, x, core), mp: 4 (over z).
Axes of the slice: x: 2, y: 2, z: 4, core: 2. Of those that a mesh axis runs over, the one named last changes fastest.
Arguments:
- tokens: bfloat16 [1024, 4096], P('seq', 'mp'), may hold values from -10 to 10
- norm_gain: float32 [4096], replicated, may hold values from 0.1 to 1.9
- w_cand: bfloat16 [4096, 4096], P('seq', 'mp'), may hold values from -0.125 to 0.125
- w_gate: bfloat16 [4096, 4096], P('seq', 'mp'), may hold values from -0.046875 to 0.046875
- rec_gate: float32 [4096], P('mp'), may hold values from -0.75 to 0.75
- rec_cand: float32 [4096], P('mp'), may hold values from -0.6 to 0.6
- bias_gate: float32 [4096], P('mp')
- w_out: bfloat16 [4096, 4096], P('mp'), may hold values from -0.09375 to 0.09375
Outputs:
- output: bfloat16 [1024, 4096], P('seq', 'mp')
All inputs are finite; a program needn't handle non-finite values.
Results may differ from a plain program's by a relative error of at most 0.0048.
Values may be sent and summed in bfloat16 or wider, within the bound.
A program may use at most 64 MiB of HBM per device.

v0:
```python
import jax
import jax.numpy as jnp
from jax import lax
from jax.sharding import PartitionSpec as P

NEWTON = 3


def prefix(value, axis, join, neutral):
    count, mine = (lax.axis_size(axis), lax.axis_index(axis))
    pieces = jax.tree.map(lambda part: lax.all_gather(part, axis), value)
    subtotal = jax.tree.map(
        lambda part, zero: jnp.full_like(part, 0) + jnp.asarray(zero, part.dtype), value, neutral
    )

    def lap(position, subtotal):
        longer = join(subtotal, jax.tree.map(lambda part: part[position], pieces))
        return jax.tree.map(lambda new, old: jnp.where(position < mine, new, old), longer, subtotal)

    return lax.fori_loop(0, count - 1, lap, subtotal)


def compose(earlier, later):
    return (later[0] * earlier[0], later[0] * earlier[1] + later[1])


def cell(previous, cand_pre, gate_pre, rec_gate, rec_cand, bias_gate):
    gate = jax.nn.sigmoid(gate_pre + rec_gate * previous + bias_gate)
    cand = jnp.tanh(cand_pre + rec_cand * previous)
    value = gate * previous + (1.0 - gate) * cand
    slope = (
        gate
        + gate * (1.0 - gate) * rec_gate * (previous - cand)
        + (1.0 - gate) * (1.0 - cand * cand) * rec_cand
    )
    return (value, slope)


def per_device(tokens, norm_gain, w_cand, w_gate, rec_gate, rec_cand, bias_gate, w_out):
    tok_rows = tokens.shape[0]
    channels = w_cand.shape[1]
    whole = lax.all_gather(tokens, "mp", axis=1, tiled=True)
    wide = whole.astype(jnp.float32)
    factor = lax.rsqrt(jnp.mean(wide * wide, axis=1, keepdims=True) + 1e-05)
    normed = (wide * factor * norm_gain).astype(jnp.bfloat16)
    cand_pre = jnp.dot(
        normed,
        lax.all_gather(w_cand, "seq", axis=0, tiled=True),
        preferred_element_type=jnp.float32,
    )
    gate_pre = jnp.dot(
        normed,
        lax.all_gather(w_gate, "seq", axis=0, tiled=True),
        preferred_element_type=jnp.float32,
    )
    state = jnp.zeros((tok_rows, channels), jnp.float32)
    carried = jnp.zeros((channels,), jnp.float32)
    ones_row = jnp.ones((channels,), jnp.float32)
    for newton_step in range(NEWTON):
        previous = jnp.concatenate([carried[None, :], state[:-1]], axis=0)
        value, slope = cell(previous, cand_pre, gate_pre, rec_gate, rec_cand, bias_gate)
        offset = value - slope * previous
        sweep_a, sweep_b = lax.associative_scan(compose, (slope, offset), axis=0)
        entering = prefix((sweep_a[-1], sweep_b[-1]), "seq", compose, (ones_row, carried * 0.0))
        carried = entering[1]
        state = sweep_a * carried + sweep_b
    state_b = state.astype(jnp.bfloat16)
    partial_sums = jnp.dot(state_b, w_out, preferred_element_type=jnp.float32)
    summed = lax.psum_scatter(partial_sums, "mp", scatter_dimension=1, tiled=True)
    return summed.astype(jnp.bfloat16)


def solution(mesh):
    placed = (
        P("seq", "mp"),
        P(),
        P("seq", "mp"),
        P("seq", "mp"),
        P("mp"),
        P("mp"),
        P("mp"),
        P("mp", None),
    )
    return jax.shard_map(
        per_device, mesh=mesh, in_specs=placed, out_specs=P("seq", "mp"), check_vma=False
    )
```

profile of v0, /device:TPU:0, one launch (start us, length us, event | category | flops | bytes accessed | tf_op | source)
XLA Modules:
  0.0 296.8 jit_solution(11191967048189579970)
XLA Ops:
  6.5 0.7 all-gather.10.cloned.1.call-update
  8.8 30.8 %all-gather.10.cloned.1.call-done = bf16[128,4096]{1,0:T(8,128)(2,1)} async-done(((bf16[128,1024]{1,0:T(8,128)(2,1)}), bf16[128,4096]{1,0:T(8,128)(2,1)}) %all-gather.10.cloned.1.call-update) | async-done | bytes 1048592 | tf_op jit(solution)/shard_map/all_gather | solution.py:42
  39.6 1.5 fusion
  41.2 54.0 %all-gather.12.cloned.1.call-done = bf16[4096,1024]{1,0:T(8,128)(2,1)} async-done(((bf16[512,1024]{1,0:T(8,128)(2,1)}), bf16[4096,1024]{1,0:T(8,128)(2,1)}) %all-gather.12.cloned.1.call-update) | async-done | bytes 8388624 | tf_op jit(solution)/shard_map/all_gather | solution.py:53
  95.2 5.0 %fusion.26 = f32[128,1024]{1,0:T(8,128)S(1)} fusion(bf16[4096,1024]{1,0:T(8,128)(2,1)} %all-gather.12.cloned.1.call-done, bf16[128,4096]{1,0:T(8,128)(2,1)} %all-gather.10.cloned.1.call-done, f32[4096]{0:T(1024)S(1)} %copy-done.5, f32[128]{0:T(128)S(1)} %add_rsqrt_fusion), kind=kOutput, calls=%fused_computation.56 | convolution fusion | flops 1075838976 | bytes 9978368 | tf_op jit(solution)/shard_map/dot_general | solution.py:51
  100.2 51.2 %all-gather.14.cloned.1.call-done = bf16[4096,1024]{1,0:T(8,128)(2,1)} async-done(((bf16[512,1024]{1,0:T(8,128)(2,1)}), bf16[4096,1024]{1,0:T(8,128)(2,1)}) %all-gather.14.cloned.1.call-update) | async-done | bytes 8388624 | tf_op jit(solution)/shard_map/all_gather | solution.py:48
  151.4 5.1 %fusion.6 = (f32[128,1024]{1,0:T(8,128)S(1)}, f32[128,1024]{1,0:T(8,128)S(1)}, f32[128,1024]{1,0:T(8,128)S(1)}) fusion(f32[1024]{0:T(1024)S(1)} %copy-done.6, f32[1024]{0:T(1024)S(1)} %get-tuple-element.441, f32[1024]{0:T(1024)S(1)} %copy-done.7, f32[1024]{0:T(1024)S(1)} %copy-done.8, f32[128,1024]{1,0:T(8,128)S(1)} %fusion.26, ...), kind=kOutput, calls=%fused_computation.26 | convolution fusion | flops 1078722560 | bytes 11571712 | tf_op jit(solution)/shard_map/dot_general | solution.py:46
  156.9 0.8 slice.660
  157.7 1.0 fusion.59
  161.4 0.8 add.628
  162.2 0.8 add_multiply_fusion.5
  163.1 1.7 pad.271
  164.9 1.7 pad.285
  166.7 0.8 add_bitcast_fusion.4
  167.5 9.1 %all-gather.1 = f32[8,1,1024]{2,1,0:T(1,128)S(1)} all-gather(f32[1,1,1024]{2,1,0:T(1,128)S(1)} %add_bitcast_fusion.4), channel_id=1, replica_groups=mesh['seq'=8,'mp'=4] {'seq'}, dimensions={0}, use_global_device_ids=true | all-gather | bytes 36864 | tf_op jit(solution)/shard_map/all_gather | solution.py:11
  176.6 0.8 add_bitcast_fusion.5
  177.4 8.2 %all-gather = f32[8,1,1024]{2,1,0:T(1,128)S(1)} all-gather(f32[1,1,1024]{2,1,0:T(1,128)S(1)} %add_bitcast_fusion.5), channel_id=1, replica_groups=mesh['seq'=8,'mp'=4] {'seq'}, dimensions={0}, use_global_device_ids=true | all-gather | bytes 36864 | tf_op jit(solution)/shard_map/all_gather | solution.py:11
  187.1 0.8 slice.727
  187.9 1.0 fusion.58
  191.7 0.8 add.663
  192.5 0.8 add_multiply_fusion.3
  193.3 1.7 pad.299
  195.1 1.7 pad.313
  197.0 0.8 add_bitcast_fusion.2
  197.7 9.2 %all-gather.3 = f32[8,1,1024]{2,1,0:T(1,128)S(1)} all-gather(f32[1,1,1024]{2,1,0:T(1,128)S(1)} %add_bitcast_fusion.2), channel_id=1, replica_groups=mesh['seq'=8,'mp'=4] {'seq'}, dimensions={0}, use_global_device_ids=true | all-gather | bytes 36864 | tf_op jit(solution)/shard_map/all_gather | solution.py:11
  207.0 0.8 add_bitcast_fusion.3
  207.8 8.2 %all-gather.2 = f32[8,1,1024]{2,1,0:T(1,128)S(1)} all-gather(f32[1,1,1024]{2,1,0:T(1,128)S(1)} %add_bitcast_fusion.3), channel_id=1, replica_groups=mesh['seq'=8,'mp'=4] {'seq'}, dimensions={0}, use_global_device_ids=true | all-gather | bytes 36864 | tf_op jit(solution)/shard_map/all_gather | solution.py:11
  220.9 9.1 %all-gather.5 = f32[8,1,1024]{2,1,0:T(1,128)S(1)} all-gather(f32[1,1,1024]{2,1,0:T(1,128)S(1)} %add_bitcast_fusion), channel_id=1, replica_groups=mesh['seq'=8,'mp'=4] {'seq'}, dimensions={0}, use_global_device_ids=true | all-gather | bytes 36864 | tf_op jit(solution)/shard_map/all_gather | solution.py:11
  230.1 8.2 %all-gather.4 = f32[8,1,1024]{2,1,0:T(1,128)S(1)} all-gather(f32[1,1,1024]{2,1,0:T(1,128)S(1)} %add_bitcast_fusion.1), channel_id=1, replica_groups=mesh['seq'=8,'mp'=4] {'seq'}, dimensions={0}, use_global_device_ids=true | all-gather | bytes 36864 | tf_op jit(solution)/shard_map/all_gather | solution.py:11
  238.7 6.1 %fusion.28 = f32[128,4096]{1,0:T(8,128)} fusion(bf16[1024,4096]{1,0:T(8,128)(2,1)} %param.21, f32[128,1024]{1,0:T(8,128)S(1)} %pad.341, f32[128,1024]{1,0:T(8,128)S(1)} %pad.342, f32[128,1024]{1,0:T(8,128)S(1)} %pad.327, f32[128,1024]{1,0:T(8,128)S(1)} %pad.328, f32[1024]{0:T(1024)S(1)} %get-tuple-element.289), kind=kOutput, calls=%fused_computation.57 | convolution fusion | flops 1074397184 | bytes 12587008 | tf_op jit(solution)/shard_map/dot_general | solution.py:68
  244.8 43.8 %reduce-scatter.2.cloned.1.call-done = f32[128,1024]{1,0:T(8,128)} async-done(((f32[128,4096]{1,0:T(8,128)}), f32[128,1024]{1,0:T(8,128)}) %reduce-scatter.2.cloned.1.call-update) | async-done | bytes 524304 | tf_op jit(solution)/shard_map/reduce_scatter | solution.py:69
  288.5 1.8 convert_element_type.15
  (394 shorter events, 13.8 us)
Async XLA Ops:
  6.5 2.3 copy-start.7
  6.5 2.3 copy-start.6
  6.5 88.7 %copy-start.5 = (f32[4096]{0:T(1024)S(1)}, f32[4096]{0:T(1024)}, u32[]{:S(2)}) copy-start(f32[4096]{0:T(1024)} %param.15) | copy-start | bytes 49156
  6.5 33.1 %all-gather.10.cloned.1.call-start = ((), (), s32[]{:S(2)}) async-start(), calls=%async_computation.1 | async-start | bytes 1310720 | tf_op jit(solution)/shard_map/all_gather | solution.py:42
  7.3 87.9 %all-gather.12.cloned.1.call-start = ((), (), s32[]{:S(2)}) async-start(), calls=%async_computation.2 | async-start | bytes 9437184 | tf_op jit(solution)/shard_map/all_gather | solution.py:53
  8.0 143.4 %all-gather.14.cloned.1.call-start = ((), (), s32[]{:S(2)}) async-start(), calls=%async_computation.3 | async-start | bytes 9437184 | tf_op jit(solution)/shard_map/all_gather | solution.py:48
  8.7 279.8 %reduce-scatter.2.cloned.1.call-start = ((), (), s32[]{:S(2)}) async-start(), calls=%async_computation.4 | async-start | bytes 2621440 | tf_op jit(solution)/shard_map/reduce_scatter | solution.py:69
  41.2 110.2 %copy-start = (bf16[128,4096]{1,0:T(8,128)(2,1)S(1)}, bf16[128,4096]{1,0:T(8,128)(2,1)}, u32[]{:S(2)}) copy-start(bf16[128,4096]{1,0:T(8,128)(2,1)} %all-gather.10.cloned.1.call-done) | copy-start | bytes 3145732
  41.2 110.2 %copy-start.8 = (f32[1024]{0:T(1024)S(1)}, f32[1024]{0:T(1024)}, u32[]{:S(2)}) copy-start(f32[1024]{0:T(1024)} %param.20) | copy-start | bytes 12292
  163.0 1.8 copy-start.3
  163.0 3.6 %copy-start.1 = (f32[64,1024]{1,0:T(8,128)S(1)}, f32[64,1024]{1,0:T(8,128)}, u32[]{:S(2)}) copy-start(f32[64,1024]{1,0:T(8,128)} %add.628) | copy-start | bytes 786436
  193.3 1.8 copy-start.4
  193.3 3.6 %copy-start.2 = (f32[64,1024]{1,0:T(8,128)S(1)}, f32[64,1024]{1,0:T(8,128)}, u32[]{:S(2)}) copy-start(f32[64,1024]{1,0:T(8,128)} %add.663) | copy-start | bytes 786436
Sparse Core Ops, SparseCore 0:
  8.9 30.6 all-gather.9
  41.5 53.6 all-gather.11
  97.1 54.2 all-gather.13
  244.9 43.6 reduce-scatter.1
where the time goes:
time: 298 us; the launch traced here: 297 us
  waiting for transfers between devices  182 us (61%)
  blocking collectives  51.9 us (17%)
  local copies, waits for them, and re-layouts  16.1 us (5%)
  matrix products  16.1 us (5%)
  between operations  15.1 us (5%)
  other arithmetic  15 us (5%)
    all_gather x1, waiting for transfers between devices, per_device(): lax.all_gather(w_gate, 'seq', axis=0, tiled=True)  54 us
    all_gather x6, blocking collectives, prefix(): pieces = jax.tree.map(lambda part: lax.all_gather(part, axis), value)  51.9 us
    all_gather x1, waiting for transfers between devices, per_device(): lax.all_gather(w_cand, 'seq', axis=0, tiled=True)  51.2 us
    reduce_scatter x1, waiting for transfers between devices, per_device(): lax.psum_scatter(partial_sums, 'mp', scatter_dimension=1, tiled=True)  43.8 us
    all_gather x1, waiting for transfers between devices, per_device(): whole = lax.all_gather(tokens, 'mp', axis=1, tiled=True)  30.8 us
    pad x68, local copies, waits for them, and re-layouts, per_device(): sweep_a, sweep_b = lax.associative_scan(compose, (slope, offset), axis=0)  8.35 us
    slice x132, local copies, waits for them, and re-layouts, per_device(): sweep_a, sweep_b = lax.associative_scan(compose, (slope, offset), axis=0)  6.86 us
    dot_general x1, matrix products, per_device(): partial_sums = jnp.dot(state_b, w_out, preferred_element_type=jnp.float32)  6.06 us
  transfers between devices with their start and end apart: 4, of which 4 were waited for; matrix products, arithmetic and copies ran while one was open for 2% of the time, Pallas kernels for 0%

commit v1 on v0

--- a/solution.py
+++ b/solution.py
@@ -4,6 +4,18 @@
 from jax.sharding import PartitionSpec as P
 
 NEWTON = 3
+
+
+def collect(x, axis, dim):
+    ways, here, lap = (lax.axis_size(axis), lax.axis_index(axis), x.shape[dim])
+    line, have = (x, 1)
+    while have < ways:
+        line = jnp.concatenate(
+            [line, lax.ppermute(line, axis, [(d, (d - have) % ways) for d in range(ways)])],
+            axis=dim,
+        )
+        have = 2 * have
+    return jnp.roll(line, here * lap, axis=dim)
 
 
 def prefix(value, axis, join, neutral):
@@ -43,11 +55,7 @@
     wide = whole.astype(jnp.float32)
     factor = lax.rsqrt(jnp.mean(wide * wide, axis=1, keepdims=True) + 1e-05)
     normed = (wide * factor * norm_gain).astype(jnp.bfloat16)
-    cand_pre = jnp.dot(
-        normed,
-        lax.all_gather(w_cand, "seq", axis=0, tiled=True),
-        preferred_element_type=jnp.float32,
-    )
+    cand_pre = jnp.dot(normed, collect(w_cand, "seq", 0), preferred_element_type=jnp.float32)
     gate_pre = jnp.dot(
         normed,
         lax.all_gather(w_gate, "seq", axis=0, tiled=True),

time: 298 us -> 367 us (1.23)
  waiting for transfers between devices: 182 us -> 225 us
  local copies, waits for them, and re-layouts: 16.1 us -> 33.8 us
  other arithmetic: 15 us -> 19.3 us
  starting transfers between devices: 0.12 us -> 4.12 us
    ppermute x0 -> x3, waiting for transfers between devices: none -> 180 us  [collect(): lax.ppermute(line, axis, [(d, (d - have) % ways) for d in range(ways)])]
    all_gather x1, waiting for transfers between devices: 54 us -> 0.01 us  [per_device(): lax.all_gather(w_gate, 'seq', axis=0, tiled=True)]
    all_gather x1 -> x0, waiting for transfers between devices: 51.2 us -> none  [per_device(): lax.all_gather(w_cand, 'seq', axis=0, tiled=True)]
    all_gather x1, waiting for transfers between devices: 30.8 us -> 0.01 us  [per_device(): whole = lax.all_gather(tokens, 'mp', axis=1, tiled=True)]
    unnamed x28 -> x37, local copies, waits for them, and re-layouts: 0.36 us -> 15.5 us
    concatenate x0 -> x2, other arithmetic: none -> 5.22 us  [collect(): jnp.concatenate([line, lax.ppermute(line, axis, [(d, (d - have) % ways) f...]
    concatenate x0 -> x1, local copies, waits for them, and re-layouts: none -> 4.56 us  [collect(): return jnp.roll(line, here * lap, axis=dim)]
    ppermute x0 -> x3, starting transfers between devices: none -> 4.04 us  [collect(): lax.ppermute(line, axis, [(d, (d - have) % ways) for d in range(ways)])]
  transfers between devices with their start and end apart: 4 -> 6, of which waited for: 4 -> 4; matrix products, arithmetic and copies ran while one was open for 2% -> 7% of each run, Pallas kernels for 0% -> 0%
where the time goes in v1:
time: 367 us; the launch traced here: 366 us
  waiting for transfers between devices  225 us (61%)
  blocking collectives  51.9 us (14%)
  local copies, waits for them, and re-layouts  33.8 us (9%)
  other arithmetic  19.3 us (5%)
  matrix products  15.8 us (4%)
  between operations  15.1 us (4%)
  starting transfers between devices  4.12 us (1%)
    ppermute x3, waiting for transfers between devices, collect(): lax.ppermute(line, axis, [(d, (d - have) % ways) for d in range(ways)])  180 us
    all_gather x6, blocking collectives, prefix(): pieces = jax.tree.map(lambda part: lax.all_gather(part, axis), value)  51.9 us
    reduce_scatter x1, waiting for transfers between devices, per_device(): lax.psum_scatter(partial_sums, 'mp', scatter_dimension=1, tiled=True)  44.1 us
    unnamed x37, local copies, waits for them, and re-layouts  15.5 us
    slice x132, local copies, waits for them, and re-layouts, per_device(): sweep_a, sweep_b = lax.associative_scan(compose, (slope, offset), axis=0)  8.1 us
  transfers between devices with their start and end apart: 6, of which 4 were waited for; matrix products, arithmetic and copies ran while one was open for 7% of the time, Pallas kernels for 0%

profile of v1, /device:TPU:0, one launch (start us, length us, event | category | flops | bytes accessed | tf_op | source)
XLA Modules:
  0.0 366.1 jit_solution(637851280416524105)
XLA Ops:
  8.1 3.4 collective-permute-start
  11.5 12.6 %collective-permute-done = bf16[512,1024]{1,0:T(8,128)(2,1)S(1)} collective-permute-done((bf16[512,1024]{1,0:T(8,128)(2,1)}, bf16[512,1024]{1,0:T(8,128)(2,1)S(1)}, u32[]{:S(2)}, u32[]{:S(2)}) %collective-permute-start) | collective-permute-done | bytes 1048608 | tf_op jit(solution)/shard_map/ppermute | solution.py:14
  24.1 1.9 pad_maximum_fusion.1
  26.6 59.0 %collective-permute-done.1 = bf16[1024,1024]{1,0:T(8,128)(2,1)S(1)} collective-permute-done((bf16[1024,1024]{1,0:T(8,128)(2,1)S(1)}, bf16[1024,1024]{1,0:T(8,128)(2,1)S(1)}, u32[]{:S(2)}, u32[]{:S(2)}) %collective-permute-start.1) | collective-permute-done | bytes 2097184 | tf_op jit(solution)/shard_map/ppermute | solution.py:14
  85.6 3.4 pad_maximum_fusion
  89.0 1.1 constant_dynamic-update-slice_fusion.7
  90.1 2.3 constant_dynamic-update-slice_fusion.6
  92.4 1.9 fusion.2
  94.3 1.5 constant_dynamic-update-slice_fusion.5
  95.8 108.3 %collective-permute-done.2 = bf16[2048,1024]{1,0:T(8,128)(2,1)} collective-permute-done((bf16[2048,1024]{1,0:T(8,128)(2,1)}, bf16[2048,1024]{1,0:T(8,128)(2,1)}, u32[]{:S(2)}, u32[]{:S(2)}) %collective-permute-start.2) | collective-permute-done | bytes 4194336 | tf_op jit(solution)/shard_map/ppermute | solution.py:14
  204.2 4.6 %constant_dynamic-update-slice_fusion.4 = bf16[8192,1024]{1,0:T(8,128)(2,1)} fusion(bf16[8192,1024]{1,0:T(8,128)(2,1)} %constant_dynamic-update-slice_fusion.5, bf16[2048,1024]{1,0:T(8,128)(2,1)} %collective-permute-done.2), kind=kLoop, calls=%fused_computation.144 | loop fusion | bytes 8388608
  208.8 1.0 constant_dynamic-update-slice_fusion.3
  209.8 1.0 constant_dynamic-update-slice_fusion.2
  210.9 1.6 constant_dynamic-update-slice_fusion.1
  212.5 4.6 %constant_dynamic-update-slice_fusion = bf16[8192,1024]{1,0:T(8,128)(2,1)} fusion(bf16[8192,1024]{1,0:T(8,128)(2,1)} %constant_dynamic-update-slice_fusion.1, bf16[2048,1024]{1,0:T(8,128)(2,1)} %collective-permute-done.2), kind=kLoop, calls=%fused_computation.140 | loop fusion | bytes 8388608 | tf_op jit(solution)/shard_map/jit(_roll_dynamic)/concatenate | solution.py:18
  217.0 4.7 %fusion.27 = f32[128,1024]{1,0:T(8,128)S(1)} fusion(bf16[4096,1024]{1,0:T(8,128)(2,1)} %all-gather.11.cloned.1.call-done, bf16[128,4096]{1,0:T(8,128)(2,1)S(1)} %copy-done.3, f32[4096]{0:T(1024)S(1)} %copy-done.6, f32[128]{0:T(128)S(1)} %add_rsqrt_fusion), kind=kOutput, calls=%fused_computation.59 | convolution fusion | flops 1075838976 | bytes 9978368 | tf_op jit(solution)/shard_map/dot_general | solution.py:59
  221.7 5.1 %fusion.8 = (f32[128,1024]{1,0:T(8,128)S(1)}, f32[128,1024]{1,0:T(8,128)S(1)}, f32[128,1024]{1,0:T(8,128)S(1)}) fusion(f32[1024]{0:T(1024)S(1)} %copy-done.7, f32[1024]{0:T(1024)S(1)} %get-tuple-element.441, f32[1024]{0:T(1024)S(1)} %copy-done.8, f32[1024]{0:T(1024)S(1)} %copy-done.9, f32[128,1024]{1,0:T(8,128)S(1)} %fusion.27, ...), kind=kOutput, calls=%fused_computation.30 | convolution fusion | flops 1078722560 | bytes 11571716 | tf_op jit(solution)/shard_map/dot_general | solution.py:58
  228.0 1.0 fusion.61
  234.6 1.7 pad.271
  237.5 1.1 pad.639
  238.6 8.2 %all-gather.1 = f32[8,1,1024]{2,1,0:T(1,128)S(1)} all-gather(f32[1,1,1024]{2,1,0:T(1,128)S(1)} %add_bitcast_fusion.4), channel_id=1, replica_groups=mesh['seq'=8,'mp'=4] {'seq'}, dimensions={0}, use_global_device_ids=true | all-gather | bytes 36864 | tf_op jit(solution)/shard_map/all_gather | solution.py:23
  247.6 9.3 %all-gather = f32[8,1,1024]{2,1,0:T(1,128)S(1)} all-gather(f32[1,1,1024]{2,1,0:T(1,128)S(1)} %add_bitcast_fusion.5), channel_id=1, replica_groups=mesh['seq'=8,'mp'=4] {'seq'}, dimensions={0}, use_global_device_ids=true | all-gather | bytes 36864 | tf_op jit(solution)/shard_map/all_gather | solution.py:23
  259.2 1.0 fusion.60
  263.9 1.7 pad.299
  265.8 1.1 pad.641
  266.9 8.2 %all-gather.3 = f32[8,1,1024]{2,1,0:T(1,128)S(1)} all-gather(f32[1,1,1024]{2,1,0:T(1,128)S(1)} %add_bitcast_fusion.2), channel_id=1, replica_groups=mesh['seq'=8,'mp'=4] {'seq'}, dimensions={0}, use_global_device_ids=true | all-gather | bytes 36864 | tf_op jit(solution)/shard_map/all_gather | solution.py:23
  275.9 9.1 %all-gather.2 = f32[8,1,1024]{2,1,0:T(1,128)S(1)} all-gather(f32[1,1,1024]{2,1,0:T(1,128)S(1)} %add_bitcast_fusion.3), channel_id=1, replica_groups=mesh['seq'=8,'mp'=4] {'seq'}, dimensions={0}, use_global_device_ids=true | all-gather | bytes 36864 | tf_op jit(solution)/shard_map/all_gather | solution.py:23
  289.8 8.2 %all-gather.5 = f32[8,1,1024]{2,1,0:T(1,128)S(1)} all-gather(f32[1,1,1024]{2,1,0:T(1,128)S(1)} %add_bitcast_fusion), channel_id=1, replica_groups=mesh['seq'=8,'mp'=4] {'seq'}, dimensions={0}, use_global_device_ids=true | all-gather | bytes 36864 | tf_op jit(solution)/shard_map/all_gather | solution.py:23
  298.2 9.1 %all-gather.4 = f32[8,1,1024]{2,1,0:T(1,128)S(1)} all-gather(f32[1,1,1024]{2,1,0:T(1,128)S(1)} %add_bitcast_fusion.1), channel_id=1, replica_groups=mesh['seq'=8,'mp'=4] {'seq'}, dimensions={0}, use_global_device_ids=true | all-gather | bytes 36864 | tf_op jit(solution)/shard_map/all_gather | solution.py:23
  307.6 6.1 %fusion.29 = f32[128,4096]{1,0:T(8,128)} fusion(bf16[1024,4096]{1,0:T(8,128)(2,1)} %param.21, f32[128,1024]{1,0:T(8,128)S(1)} %pad.341, f32[128,1024]{1,0:T(8,128)S(1)} %pad.342, f32[128,1024]{1,0:T(8,128)S(1)} %pad.327, f32[128,1024]{1,0:T(8,128)S(1)} %pad.328, f32[1024]{0:T(1024)S(1)} %get-tuple-element.289), kind=kOutput, calls=%fused_computation.60 | convolution fusion | flops 1074397184 | bytes 12587008 | tf_op jit(solution)/shard_map/dot_general | solution.py:76
  313.7 44.1 %reduce-scatter.2.cloned.1.call-done = f32[128,1024]{1,0:T(8,128)} async-done(((f32[128,4096]{1,0:T(8,128)}), f32[128,1024]{1,0:T(8,128)}) %reduce-scatter.2.cloned.1.call-update) | async-done | bytes 524304 | tf_op jit(solution)/shard_map/reduce_scatter | solution.py:77
  357.8 1.8 convert_element_type.15
  (409 shorter events, 22.1 us)
Async XLA Ops:
  6.5 82.4 %copy-start = (bf16[512,1024]{1,0:T(8,128)(2,1)S(1)}, bf16[512,1024]{1,0:T(8,128)(2,1)}, u32[]{:S(2)}) copy-start(bf16[512,1024]{1,0:T(8,128)(2,1)} %param.16) | copy-start | bytes 3145732
  6.5 83.5 %copy-start.8 = (f32[1024]{0:T(1024)S(1)}, f32[1024]{0:T(1024)}, u32[]{:S(2)}) copy-start(f32[1024]{0:T(1024)} %param.18) | copy-start | bytes 12292
  6.5 83.5 %copy-start.7 = (f32[1024]{0:T(1024)S(1)}, f32[1024]{0:T(1024)}, u32[]{:S(2)}) copy-start(f32[1024]{0:T(1024)} %param.19) | copy-start | bytes 12292
  6.5 85.8 %all-gather.9.cloned.1.call-start = ((), (), s32[]{:S(2)}) async-start(), calls=%async_computation.1 | async-start | bytes 1310720 | tf_op jit(solution)/shard_map/all_gather | solution.py:54
  7.3 209.8 %all-gather.11.cloned.1.call-start = ((), (), s32[]{:S(2)}) async-start(), calls=%async_computation.2 | async-start | bytes 9437184 | tf_op jit(solution)/shard_map/all_gather | solution.py:61
  8.0 349.8 %reduce-scatter.2.cloned.1.call-start = ((), (), s32[]{:S(2)}) async-start(), calls=%async_computation.3 | async-start | bytes 2621440 | tf_op jit(solution)/shard_map/reduce_scatter | solution.py:77
  8.1 16.0 %collective-permute-start = (bf16[512,1024]{1,0:T(8,128)(2,1)}, bf16[512,1024]{1,0:T(8,128)(2,1)S(1)}, u32[]{:S(2)}, u32[]{:S(2)}) collective-permute-start(bf16[512,1024]{1,0:T(8,128)(2,1)} %param.16), channel_id=1, source_target_pairs={{0,28},{4,0},{8,4},{12,8},{16,12},{20,16},{24,20},{28,24},{1,29},{... | collective-permute-start | bytes 3145736 | tf_op jit(solution)/shard_map/ppermute | solution.py:14
  24.1 61.5 %copy-start.1 = (bf16[512,1024]{1,0:T(8,128)(2,1)}, bf16[512,1024]{1,0:T(8,128)(2,1)S(1)}, u32[]{:S(2)}) copy-start(bf16[512,1024]{1,0:T(8,128)(2,1)S(1)} %collective-permute-done) | copy-start | bytes 3145732
  26.0 59.6 %collective-permute-start.1 = (bf16[1024,1024]{1,0:T(8,128)(2,1)S(1)}, bf16[1024,1024]{1,0:T(8,128)(2,1)S(1)}, u32[]{:S(2)}, u32[]{:S(2)}) collective-permute-start(bf16[1024,1024]{1,0:T(8,128)(2,1)S(1)} %pad_maximum_fusion.1), channel_id=1, source_target_pairs={{0,24},{4,28},{8,0},{12,4},{16,8},{20,12},{24,16},{28,20},{1,25},{... | collective-permute-start | bytes 6291464 | tf_op jit(solution)/shard_map/ppermute | solution.py:14
  89.0 115.2 %collective-permute-start.2 = (bf16[2048,1024]{1,0:T(8,128)(2,1)}, bf16[2048,1024]{1,0:T(8,128)(2,1)}, u32[]{:S(2)}, u32[]{:S(2)}) collective-permute-start(bf16[2048,1024]{1,0:T(8,128)(2,1)} %pad_maximum_fusion), channel_id=1, source_target_pairs={{0,16},{4,20},{8,24},{12,28},{16,0},{20,4},{24,8},{28,12},{1,17},{... | collective-permute-start | bytes 12582920 | tf_op jit(solution)/shard_map/ppermute | solution.py:14
  92.4 117.5 %copy-start.2 = (bf16[512,1024]{1,0:T(8,128)(2,1)S(1)}, bf16[512,1024]{1,0:T(8,128)(2,1)}, u32[]{:S(2)}) copy-start(bf16[512,1024]{1,0:T(8,128)(2,1)} %copy-done.1) | copy-start | bytes 3145732
  208.8 8.2 %copy-start.6 = (f32[4096]{0:T(1024)S(1)}, f32[4096]{0:T(1024)}, u32[]{:S(2)}) copy-start(f32[4096]{0:T(1024)} %param.15) | copy-start | bytes 49156
  209.8 7.2 %copy-start.3 = (bf16[128,4096]{1,0:T(8,128)(2,1)S(1)}, bf16[128,4096]{1,0:T(8,128)(2,1)}, u32[]{:S(2)}) copy-start(bf16[128,4096]{1,0:T(8,128)(2,1)} %all-gather.9.cloned.1.call-done) | copy-start | bytes 3145732
  217.0 4.7 %copy-start.9 = (f32[1024]{0:T(1024)S(1)}, f32[1024]{0:T(1024)}, u32[]{:S(2)}) copy-start(f32[1024]{0:T(1024)} %param.20) | copy-start | bytes 12292
  232.0 1.8 copy-start.4
  232.0 1.8 copy-start.5
Sparse Core Ops, SparseCore 0:
  8.9 30.6 all-gather.8
  41.5 99.3 all-gather.10
  313.8 43.9 reduce-scatter.1
